TPU v7x, 32 devices: a whole 2x2x4 slice. The times are simulated.
32 devices in a mesh: rows: 16 (over z, x, core), cols: 2 (over y).
Axes of the slice: x: 2, y: 2, z: 4, core: 2. Of those that a mesh axis runs over, the one named last changes fastest.
Arguments:
- slab: float32 [131072, 512], P('rows', 'cols')
- sign_bits: int32 [131072], P('rows'), may hold values from 0 to 1
- block_mask: int32 [1024], P('rows'), may hold values 0 or 1
- sample_rows: int32 [2048], P('rows'), may hold values from 0 to 8191, as said below
Outputs:
- sketch_rows: float32 [2048, 512], P('rows', 'cols')
- r_factor: float32 [512, 512], P(None, 'cols')
Inputs may be any that keep to these rules, and one draw needn't show every extreme that they name: `sample_rows`: each block of 128 entries names rows of the matching index of rows, as numbers below 8192; rows may repeat.
All inputs are finite; a program needn't handle non-finite values. No bound on the sum of `block_mask` on one device may be relied on, other than what follows from the above.
Results may differ from a plain program's by a relative error of at most 0.00016.
Values sent between devices are 32-bit elements; how exact they have to be, the bound alone decides.
No kernel may reach another device: no remote copies, remote signals or barrier semaphores. Data moves between devices by JAX's collectives and lax.ppermute only.
A program may use at most 64 MiB of HBM per device.

v0:
```python
import math
import jax
import jax.numpy as jnp
from jax import lax
from jax.sharding import PartitionSpec as P


def swapped(value, axis, bit):
    return lax.ppermute(value, axis, [(i, i ^ 1 << bit) for i in range(lax.axis_size(axis))])


def bit_parity(values, bit_total):
    total = jnp.zeros(values.shape, jnp.int32)
    for position in range(bit_total):
        total = total + jnp.bitwise_and(jnp.right_shift(values, position), 1)
    return jnp.bitwise_and(total, 1)


def sylvester(order_size):
    counter = jnp.arange(order_size, dtype=jnp.int32)
    common = jnp.bitwise_and(counter[:, None], counter[None, :])
    parity = bit_parity(common, max(order_size.bit_length(), 1))
    return (1 - 2 * parity).astype(jnp.float32)


def local_mix(scaled):
    block_count = scaled.shape[0]
    block_rows = scaled.shape[1]
    first_pass = jnp.einsum(
        "jb,rbc->rjc", sylvester(block_rows), scaled, precision=lax.Precision.HIGHEST
    )
    return jnp.einsum(
        "ir,rjc->ijc", sylvester(block_count), first_pass, precision=lax.Precision.HIGHEST
    )


def body(slab, sign_bits, block_mask, sample_rows):
    row_count, panel_width = slab.shape
    groups = lax.axis_size("rows")
    block_count = block_mask.shape[0]
    block_rows = row_count // block_count
    norm_scale = 1.0 / math.sqrt(row_count * groups)
    sign_values = (2 * sign_bits - 1).astype(jnp.float32)
    mask_values = block_mask.astype(jnp.float32)
    scaled = slab.reshape(block_count, block_rows, panel_width) * sign_values.reshape(
        block_count, block_rows, 1
    )
    scaled = scaled * mask_values.reshape(block_count, 1, 1)
    mixed_rows = local_mix(scaled).reshape(row_count, panel_width)
    pick_count = sample_rows.shape[0]
    device = lax.axis_index("rows")
    for bit_level in range(groups.bit_length() - 1):
        partner = swapped(mixed_rows, "rows", bit_level)
        high_bit = jnp.bitwise_and(jnp.right_shift(device, bit_level), 1)
        mixed_rows = jnp.where(high_bit == 0, mixed_rows + partner, partner - mixed_rows)
    sketch = jnp.take(mixed_rows, sample_rows, axis=0) * norm_scale
    full_rows = lax.all_gather(sketch, "cols", axis=1, tiled=True)
    panel_index = lax.axis_index("cols")
    local_gram = jnp.einsum("sa,sb->ab", full_rows, full_rows, precision=lax.Precision.HIGHEST)
    gram_matrix = lax.psum(local_gram, "rows")
    gram_matrix = gram_matrix / (pick_count * groups)
    lower_factor = jnp.linalg.cholesky(gram_matrix)
    upper_factor = lower_factor.T
    r_panel = lax.dynamic_slice_in_dim(upper_factor, panel_index * panel_width, panel_width, 1)
    return (sketch, r_panel)


def solution(mesh):
    in_specs = (P("rows", "cols"), P("rows"), P("rows"), P("rows"))
    out_specs = (P("rows", "cols"), P(None, "cols"))
    return jax.shard_map(body, mesh=mesh, in_specs=in_specs, out_specs=out_specs, check_vma=False)
```

profile of v0, /device:TPU:0, one launch (start us, length us, event | category | flops | bytes accessed | tf_op | source)
XLA Modules:
  0.0 1038.9 jit_solution(15961802083530760773)
XLA Ops:
  7.2 0.0 all-reduce.3.cloned.1.call-start
  7.2 0.8 convert_bitcast_fusion
  8.0 0.7 convert_element_type.14
  8.6 19.1 %fusion.2 = f32[64,256,128]{2,1,0:T(8,128)} fusion(f32[64,128,256]{2,1,0:T(8,128)} %bitcast.40, f32[64]{0:T(128)S(1)} %convert_element_type.14, f32[64,128]{1,0:T(8,128)S(1)} %convert_bitcast_fusion), kind=kOutput, calls=%fused_computation.7 | convolution fusion | flops 3225878528 | bytes 16810240 | tf_op jit(solution)/shard_map/jb,rbc->rjc/dot_general | solution.py:29
  27.8 9.2 copy.13
  36.9 10.5 %fusion = f32[64,128,256]{2,0,1:T(8,128)S(1)} fusion(f32[64,256,128]{1,0,2:T(8,128)} %copy.13), kind=kOutput, calls=%fused_computation.1 | convolution fusion | flops 1610715136 | bytes 16777216 | tf_op jit(solution)/shard_map/ir,rjc->ijc/dot_general | solution.py:32
  47.5 8.1 copy.9
  55.5 0.5 collective-permute-start
  56.0 13.1 %collective-permute-done = f32[8192,256]{1,0:T(8,128)} collective-permute-done((f32[8192,256]{1,0:T(8,128)}, f32[8192,256]{1,0:T(8,128)}, u32[]{:S(2)}, u32[]{:S(2)}) %collective-permute-start) | collective-permute-done | bytes 8388640 | tf_op jit(solution)/shard_map/ppermute | solution.py:9
  69.1 10.1 subtract_select_fusion.3
  79.2 2.9 collective-permute-start.1
  82.0 181.1 %collective-permute-done.1 = f32[8192,256]{1,0:T(8,128)} collective-permute-done((f32[8192,256]{1,0:T(8,128)}, f32[8192,256]{1,0:T(8,128)}, u32[]{:S(2)}, u32[]{:S(2)}) %collective-permute-start.1) | collective-permute-done | bytes 8388640 | tf_op jit(solution)/shard_map/ppermute | solution.py:9
  263.1 10.1 subtract_select_fusion.2
  273.2 1.8 collective-permute-start.2
  275.0 180.5 %collective-permute-done.2 = f32[8192,256]{1,0:T(8,128)} collective-permute-done((f32[8192,256]{1,0:T(8,128)}, f32[8192,256]{1,0:T(8,128)}, u32[]{:S(2)}, u32[]{:S(2)}) %collective-permute-start.2) | collective-permute-done | bytes 8388640 | tf_op jit(solution)/shard_map/ppermute | solution.py:9
  455.5 10.1 subtract_select_fusion.1
  465.5 2.5 collective-permute-start.3
  468.1 359.5 %collective-permute-done.3 = f32[8192,256]{1,0:T(8,128)} collective-permute-done((f32[8192,256]{1,0:T(8,128)}, f32[8192,256]{1,0:T(8,128)}, u32[]{:S(2)}, u32[]{:S(2)}) %collective-permute-start.3) | collective-permute-done | bytes 8388640 | tf_op jit(solution)/shard_map/ppermute | solution.py:9
  827.6 10.1 subtract_select_fusion
  837.7 4.1 gather_fusion
  841.8 0.1 select_multiply_fusion
  841.9 0.0 copy-start
  841.9 5.8 all_gather.3
  847.7 2.1 fusion.110
  849.8 0.0 all-reduce.3.cloned.1.call-update
  849.8 94.5 %all-reduce.3.cloned.1.call-done = f32[512,512]{0,1:T(8,128)} async-done(((f32[512,512]{0,1:T(8,128)}), f32[512,512]{0,1:T(8,128)}) %all-reduce.3.cloned.1.call-update) | async-done | bytes 1048592 | tf_op jit(solution)/shard_map/psum | solution.py:60
  944.3 1.3 broadcast_multiply_fusion
  945.6 0.3 copy.11
  946.0 1.5 fusion.7
  947.5 11.7 %cholesky.104 = f32[128,128]{1,0:T(8,128)S(1)} custom-call(f32[128,128]{1,0:T(8,128)S(1)} %cholesky.266), custom_call_target="Cholesky" | custom-call | tf_op jit(solution)/shard_map/jit(cholesky)/cholesky | solution.py:62
  959.2 0.1 cholesky.224
  959.3 9.8 custom-call.27
  969.2 0.3 constant_dynamic-update-slice_fusion.1
  969.5 0.3 convolution_subtract_fusion
  969.8 11.9 %cholesky.217 = f32[128,128]{1,0:T(8,128)S(1)} custom-call(f32[128,128]{1,0:T(8,128)S(1)} %cholesky.270), custom_call_target="Cholesky" | custom-call | tf_op jit(solution)/shard_map/jit(cholesky)/cholesky | solution.py:62
  981.8 9.8 custom-call.28
  991.6 0.3 convolution_dynamic-update-slice_fusion
  991.9 0.4 convolution_subtract_fusion.1
  992.3 11.7 %cholesky.238 = f32[128,128]{1,0:T(8,128)S(1)} custom-call(f32[128,128]{1,0:T(8,128)S(1)} %cholesky.275), custom_call_target="Cholesky" | custom-call | tf_op jit(solution)/shard_map/jit(cholesky)/cholesky | solution.py:62
  1004.0 0.7 compare_reduce_fusion.1
  1004.7 9.8 custom-call.29
  1014.6 0.2 convolution_dynamic-update-slice_fusion.1
  1014.8 0.4 convolution_subtract_fusion.2
  1015.2 11.7 %cholesky.255 = f32[128,128]{1,0:T(8,128)S(1)} custom-call(f32[128,128]{1,0:T(8,128)S(1)} %convolution_subtract_fusion.2), custom_call_target="Cholesky" | custom-call | tf_op jit(solution)/shard_map/jit(cholesky)/cholesky | solution.py:62
  1026.9 0.6 compare_reduce_fusion
  1027.5 0.7 compare_reduce_fusion.2
  1030.7 0.1 fusion.9
  1030.8 1.0 copy.12
  (13 shorter events, 0.2 us)
Async XLA Ops:
  7.2 937.2 %all-reduce.3.cloned.1.call-start = ((), (), s32[]{:S(2)}) async-start(), calls=%async_computation | async-start | bytes 2097152 | tf_op jit(solution)/shard_map/psum | solution.py:60
  55.5 13.6 %collective-permute-start = (f32[8192,256]{1,0:T(8,128)}, f32[8192,256]{1,0:T(8,128)}, u32[]{:S(2)}, u32[]{:S(2)}) collective-permute-start(f32[8192,256]{1,0:T(8,128)} %bitcast.5), channel_id=1, source_target_pairs={{0,2},{2,0},{4,6},{6,4},{8,10},{10,8},{12,14},{14,12},{16,18},{18,... | collective-permute-start | bytes 25165832 | tf_op jit(solution)/shard_map/ppermute | solution.py:9
  79.2 183.9 %collective-permute-start.1 = (f32[8192,256]{1,0:T(8,128)}, f32[8192,256]{1,0:T(8,128)}, u32[]{:S(2)}, u32[]{:S(2)}) collective-permute-start(f32[8192,256]{1,0:T(8,128)} %subtract_select_fusion.3), channel_id=1, source_target_pairs={{0,4},{2,6},{4,0},{6,2},{8,12},{10,14},{12,8},{14,10},{16,20},{18,... | collective-permute-start | bytes 25165832 | tf_op jit(solution)/shard_map/ppermute | solution.py:9
  273.2 182.3 %collective-permute-start.2 = (f32[8192,256]{1,0:T(8,128)}, f32[8192,256]{1,0:T(8,128)}, u32[]{:S(2)}, u32[]{:S(2)}) collective-permute-start(f32[8192,256]{1,0:T(8,128)} %subtract_select_fusion.2), channel_id=1, source_target_pairs={{0,8},{2,10},{4,12},{6,14},{8,0},{10,2},{12,4},{14,6},{16,24},{18,... | collective-permute-start | bytes 25165832 | tf_op jit(solution)/shard_map/ppermute | solution.py:9
  275.0 193.1 %copy-start.1 = (s32[128]{0:T(128)S(1)}, s32[128]{0:T(128)}, u32[]{:S(2)}) copy-start(s32[128]{0:T(128)} %param.7) | copy-start | bytes 1540
  465.5 362.1 %collective-permute-start.3 = (f32[8192,256]{1,0:T(8,128)}, f32[8192,256]{1,0:T(8,128)}, u32[]{:S(2)}, u32[]{:S(2)}) collective-permute-start(f32[8192,256]{1,0:T(8,128)} %subtract_select_fusion.1), channel_id=1, source_target_pairs={{0,16},{2,18},{4,20},{6,22},{8,24},{10,26},{12,28},{14,30},{16,0},... | collective-permute-start | bytes 25165832 | tf_op jit(solution)/shard_map/ppermute | solution.py:9
  841.9 189.9 %copy-start = (f32[128,256]{1,0:T(8,128)}, f32[128,256]{1,0:T(8,128)S(1)}, u32[]{:S(2)}) copy-start(f32[128,256]{1,0:T(8,128)S(1)} %select_multiply_fusion) | copy-start | bytes 393220
Sparse Core Ops, SparseCore 0:
  849.9 94.3 all-reduce.2
where the time goes:
time: 1050 us; the launch traced here: 1040 us
  waiting for transfers between devices  829 us (79%)
  other arithmetic  123 us (12%)
  matrix products  33.6 us (3%)
  local copies, waits for them, and re-layouts  22.9 us (2%)
  between operations  17 us (2%)
    ppermute x4, waiting for transfers between devices, swapped(): lax.ppermute(value, axis, [(i, i ^ 1 << bit) for i in range(lax.axis_size...  734 us
    psum x1, waiting for transfers between devices, body(): gram_matrix = lax.psum(local_gram, 'rows')  94.5 us
    another operation x14, other arithmetic, body(): lower_factor = jnp.linalg.cholesky(gram_matrix)  78.6 us
    select_n x4, other arithmetic, body(): jnp.where(high_bit == 0, mixed_rows + partner, partner - mixed_rows)  40.3 us
  transfers between devices with their start and end apart: 5, of which 5 were waited for; matrix products, arithmetic and copies ran while one was open for 0% of the time, Pallas kernels for 0%

commit v1 on v0

--- a/solution.py
+++ b/solution.py
@@ -57,7 +57,7 @@
     full_rows = lax.all_gather(sketch, "cols", axis=1, tiled=True)
     panel_index = lax.axis_index("cols")
     local_gram = jnp.einsum("sa,sb->ab", full_rows, full_rows, precision=lax.Precision.HIGHEST)
-    gram_matrix = lax.psum(local_gram, "rows")
+    gram_matrix = jnp.sum(lax.all_gather(local_gram, "rows"), axis=0)
     gram_matrix = gram_matrix / (pick_count * groups)
     lower_factor = jnp.linalg.cholesky(gram_matrix)
     upper_factor = lower_factor.T

time: 1050 us -> 1080 us (1.029)
  waiting for transfers between devices: 829 us -> 862 us
    all_gather x0 -> x1, waiting for transfers between devices: none -> 128 us  [body(): gram_matrix = jnp.sum(lax.all_gather(local_gram, 'rows'), axis=0)]
    psum x1 -> x0, waiting for transfers between devices: 94.5 us -> none  [body(): gram_matrix = lax.psum(local_gram, 'rows')]
where the time goes in v1:
time: 1080 us
  waiting for transfers between devices  862 us (80%)
  other arithmetic  127 us (12%)
  local copies, waits for them, and re-layouts  31.9 us (3%)
  matrix products  25.4 us (2%)
  between operations  17 us (2%)
    ppermute x4, waiting for transfers between devices, swapped(): lax.ppermute(value, axis, [(i, i ^ 1 << bit) for i in range(lax.axis_size...  734 us
    all_gather x1, waiting for transfers between devices, body(): gram_matrix = jnp.sum(lax.all_gather(local_gram, 'rows'), axis=0)  128 us
    another operation x14, other arithmetic, body(): lower_factor = jnp.linalg.cholesky(gram_matrix)  78.9 us
    select_n x4, other arithmetic, body(): jnp.where(high_bit == 0, mixed_rows + partner, partner - mixed_rows)  40.3 us
  transfers between devices with their start and end apart: 5, of which 5 were waited for; matrix products, arithmetic and copies ran while one was open for 0% of the time, Pallas kernels for 0%

profile of v1, /device:TPU:0, one launch (start us, length us, event | category | flops | bytes accessed | tf_op | source)
XLA Modules:
  0.0 1077.7 jit_solution(13816487066855370113)
XLA Ops:
  7.2 0.0 all-gather.3.cloned.1.call-start
  7.2 0.0 copy-start.1
  7.2 9.0 copy.11
  16.3 10.9 %fusion.5 = f32[64,128,256]{1,2,0:T(8,128)} fusion(f32[64,128,256]{1,2,0:T(8,128)} %copy.11, f32[64]{0:T(128)S(1)} %convert_element_type.14, f32[64,128]{1,0:T(8,128)S(1)} %convert_bitcast_fusion), kind=kOutput, calls=%fused_computation.10 | convolution fusion | flops 3225878528 | bytes 16810240 | tf_op jit(solution)/shard_map/jb,rbc->rjc/dot_general | solution.py:29
  27.2 9.2 copy.12
  36.4 10.6 fusion.53
  47.0 8.1 copy.13
  55.0 0.5 collective-permute-start
  55.5 13.1 %collective-permute-done = f32[8192,256]{1,0:T(8,128)} collective-permute-done((f32[8192,256]{1,0:T(8,128)}, f32[8192,256]{1,0:T(8,128)}, u32[]{:S(2)}, u32[]{:S(2)}) %collective-permute-start) | collective-permute-done | bytes 8388640 | tf_op jit(solution)/shard_map/ppermute | solution.py:9
  68.6 10.1 subtract_select_fusion.3
  78.7 2.9 collective-permute-start.1
  81.5 181.1 %collective-permute-done.1 = f32[8192,256]{1,0:T(8,128)} collective-permute-done((f32[8192,256]{1,0:T(8,128)}, f32[8192,256]{1,0:T(8,128)}, u32[]{:S(2)}, u32[]{:S(2)}) %collective-permute-start.1) | collective-permute-done | bytes 8388640 | tf_op jit(solution)/shard_map/ppermute | solution.py:9
  262.6 10.1 subtract_select_fusion.2
  272.7 1.8 collective-permute-start.2
  274.5 180.5 %collective-permute-done.2 = f32[8192,256]{1,0:T(8,128)} collective-permute-done((f32[8192,256]{1,0:T(8,128)}, f32[8192,256]{1,0:T(8,128)}, u32[]{:S(2)}, u32[]{:S(2)}) %collective-permute-start.2) | collective-permute-done | bytes 8388640 | tf_op jit(solution)/shard_map/ppermute | solution.py:9
  455.0 10.1 subtract_select_fusion.1
  465.0 2.5 collective-permute-start.3
  467.6 359.5 %collective-permute-done.3 = f32[8192,256]{1,0:T(8,128)} collective-permute-done((f32[8192,256]{1,0:T(8,128)}, f32[8192,256]{1,0:T(8,128)}, u32[]{:S(2)}, u32[]{:S(2)}) %collective-permute-start.3) | collective-permute-done | bytes 8388640 | tf_op jit(solution)/shard_map/ppermute | solution.py:9
  827.1 10.1 subtract_select_fusion
  837.2 4.1 gather_fusion
  841.3 0.1 select_multiply_fusion
  841.4 0.0 copy-start
  841.4 5.8 all_gather.9
  847.2 2.0 fusion.112
  849.3 0.0 all-gather.3.cloned.1.call-update
  849.3 128.2 %all-gather.3.cloned.1.call-done = f32[8192,512]{1,0:T(8,128)} async-done(((f32[512,512]{1,0:T(8,128)}), f32[8192,512]{1,0:T(8,128)}) %all-gather.3.cloned.1.call-update) | async-done | bytes 16777232 | tf_op jit(solution)/shard_map/all_gather | solution.py:60
  977.5 7.9 reduce_sum.11
  985.5 0.3 copy.14
  985.8 0.2 fusion.8
  986.0 11.7 %cholesky.104 = f32[128,128]{1,0:T(8,128)S(1)} custom-call(f32[128,128]{1,0:T(8,128)S(1)} %cholesky.266), custom_call_target="Cholesky" | custom-call | tf_op jit(solution)/shard_map/jit(cholesky)/cholesky | solution.py:62
  997.8 0.1 cholesky.224
  997.9 9.8 custom-call.27
  1007.7 0.3 constant_dynamic-update-slice_fusion.1
  1008.1 0.3 convolution_subtract_fusion
  1008.4 11.9 %cholesky.217 = f32[128,128]{1,0:T(8,128)S(1)} custom-call(f32[128,128]{1,0:T(8,128)S(1)} %cholesky.270), custom_call_target="Cholesky" | custom-call | tf_op jit(solution)/shard_map/jit(cholesky)/cholesky | solution.py:62
  1020.4 9.8 custom-call.28
  1030.2 0.3 convolution_dynamic-update-slice_fusion
  1030.4 0.4 convolution_subtract_fusion.1
  1030.8 11.7 %cholesky.238 = f32[128,128]{1,0:T(8,128)S(1)} custom-call(f32[128,128]{1,0:T(8,128)S(1)} %cholesky.275), custom_call_target="Cholesky" | custom-call | tf_op jit(solution)/shard_map/jit(cholesky)/cholesky | solution.py:62
  1042.6 0.7 compare_reduce_fusion.1
  1043.3 9.8 custom-call.29
  1053.1 0.2 convolution_dynamic-update-slice_fusion.1
  1053.3 0.4 convolution_subtract_fusion.2
  1053.7 11.9 %cholesky.255 = f32[128,128]{1,0:T(8,128)S(1)} custom-call(f32[128,128]{1,0:T(8,128)S(1)} %convolution_subtract_fusion.2), custom_call_target="Cholesky" | custom-call | tf_op jit(solution)/shard_map/jit(cholesky)/cholesky | solution.py:62
  1065.7 0.6 compare_reduce_fusion
  1066.3 0.7 compare_reduce_fusion.2
  1069.5 0.1 fusion.10
  1069.6 1.0 copy.15
  (18 shorter events, 0.2 us)
Async XLA Ops:
  7.2 970.4 %all-gather.3.cloned.1.call-start = ((), (), s32[]{:S(2)}) async-start(), calls=%async_computation | async-start | bytes 17825792 | tf_op jit(solution)/shard_map/all_gather | solution.py:60
  7.2 9.0 copy-start.1
  7.2 9.0 copy-start.2
  55.0 13.6 %collective-permute-start = (f32[8192,256]{1,0:T(8,128)}, f32[8192,256]{1,0:T(8,128)}, u32[]{:S(2)}, u32[]{:S(2)}) collective-permute-start(f32[8192,256]{1,0:T(8,128)} %bitcast.5), channel_id=1, source_target_pairs={{0,2},{2,0},{4,6},{6,4},{8,10},{10,8},{12,14},{14,12},{16,18},{18,... | collective-permute-start | bytes 25165832 | tf_op jit(solution)/shard_map/ppermute | solution.py:9
  78.7 183.9 %collective-permute-start.1 = (f32[8192,256]{1,0:T(8,128)}, f32[8192,256]{1,0:T(8,128)}, u32[]{:S(2)}, u32[]{:S(2)}) collective-permute-start(f32[8192,256]{1,0:T(8,128)} %subtract_select_fusion.3), channel_id=1, source_target_pairs={{0,4},{2,6},{4,0},{6,2},{8,12},{10,14},{12,8},{14,10},{16,20},{18,... | collective-permute-start | bytes 25165832 | tf_op jit(solution)/shard_map/ppermute | solution.py:9
  272.7 182.3 %collective-permute-start.2 = (f32[8192,256]{1,0:T(8,128)}, f32[8192,256]{1,0:T(8,128)}, u32[]{:S(2)}, u32[]{:S(2)}) collective-permute-start(f32[8192,256]{1,0:T(8,128)} %subtract_select_fusion.2), channel_id=1, source_target_pairs={{0,8},{2,10},{4,12},{6,14},{8,0},{10,2},{12,4},{14,6},{16,24},{18,... | collective-permute-start | bytes 25165832 | tf_op jit(solution)/shard_map/ppermute | solution.py:9
  274.5 193.1 %copy-start.3 = (s32[128]{0:T(128)S(1)}, s32[128]{0:T(128)}, u32[]{:S(2)}) copy-start(s32[128]{0:T(128)} %param.7) | copy-start | bytes 1540
  465.0 362.1 %collective-permute-start.3 = (f32[8192,256]{1,0:T(8,128)}, f32[8192,256]{1,0:T(8,128)}, u32[]{:S(2)}, u32[]{:S(2)}) collective-permute-start(f32[8192,256]{1,0:T(8,128)} %subtract_select_fusion.1), channel_id=1, source_target_pairs={{0,16},{2,18},{4,20},{6,22},{8,24},{10,26},{12,28},{14,30},{16,0},... | collective-permute-start | bytes 25165832 | tf_op jit(solution)/shard_map/ppermute | solution.py:9
  841.4 144.0 %copy-start = (f32[128,256]{1,0:T(8,128)}, f32[128,256]{1,0:T(8,128)S(1)}, u32[]{:S(2)}) copy-start(f32[128,256]{1,0:T(8,128)S(1)} %select_multiply_fusion) | copy-start | bytes 393220
Sparse Core Ops, SparseCore 0:
  849.4 128.0 all-gather.2
